TPU v7x, 32 devices: a whole 2x2x4 slice. The times are simulated.
32 devices in a mesh: wide: 8 (over z, core), narrow: 4 (over y, x).
Axes of the slice: x: 2, y: 2, z: 4, core: 2. Of those that a mesh axis runs over, the one named last changes fastest.
Arguments:
- traction: float32 [3, 64, 49152], P(None, None, ('wide', 'narrow')), may hold values from -6 to 6
- near_kernel: bfloat16 [96, 4, 512, 512], P(('wide', 'narrow')), may hold values from -0.125 to 0.125
- neighbours: int32 [96, 4], P(('wide', 'narrow')), may hold values from 0 to 95, as said below
- far_basis: bfloat16 [5, 49152, 128], P(None, ('wide', 'narrow')), may hold values from -4 to 4
- surface_gap: float32 [3, 49152], P(None, ('wide', 'narrow')), may hold values from -3 to 3
- friction: float32 [49152], P(('wide', 'narrow')), may hold values from 0.2 to 1
- contact_flags: int32 [49152], P(('wide', 'narrow')), may hold values 0 or 1
- cluster_order: int32 [49152], P(('wide', 'narrow')), may hold values from 0 to 49151, as said below
- approach: float32 [3, 64], replicated, may hold values from -1 to 2
Outputs:
- traction_new: float32 [3, 64, 49152], P(None, None, ('wide', 'narrow'))
- residual: float32 [3, 64, 49152], P(None, None, ('wide', 'narrow'))
- step_size: float32 [64], replicated
Inputs may be any that keep to these rules, and one draw needn't show every extreme that they name: `neighbours`: entry 0 of row b is b itself; the other 3 entries are distinct blocks other than b, each within 3 blocks of b. `cluster_order`: a permutation of the panels that maps every aligned group of 1536 panels onto itself.
All inputs are finite; a program needn't handle non-finite values. No bound on the sum of `contact_flags` on one device may be relied on, other than what follows from the above.
Results may differ from a plain program's by a relative error of at most 0.0034.
Values may be sent and summed in bfloat16 or wider, within the bound.
A program may use at most 64 MiB of HBM per device.

v0:
```python
import math
import jax
import jax.numpy as jnp
from jax import lax
from jax.sharding import PartitionSpec as P

SLIP_EPS = 0.01


def extended(cells, sides, width):
    for axis, dim in sides:
        count = lax.axis_size(axis)
        ends = count - 1
        head = lax.slice_in_dim(cells, 0, width, axis=dim)
        tail = lax.slice_in_dim(cells, cells.shape[dim] - width, cells.shape[dim], axis=dim)
        cells = jnp.concatenate(
            [
                lax.ppermute(tail, axis, [(i, (i + 1) % count) for i in range(ends)]),
                cells,
                lax.ppermute(head, axis, [((i + 1) % count, i) for i in range(ends)]),
            ],
            axis=dim,
        )
    return cells


def from_partner(block, axis, stride):
    count = lax.axis_size(axis)
    route = []
    for low in range(count):
        high = low | 1 << stride
        if high != low and high < count:
            route += [(low, high), (high, low)]
    return lax.ppermute(block, axis, route)


def near_field(field_low, near_kernel, neighbours):
    row_count, panel_count = field_low.shape
    blk_dev = near_kernel.shape[0]
    block_len = near_kernel.shape[2]
    padded = extended(field_low, ((("wide", "narrow"), 1),), panel_count)
    blocks = padded.reshape(row_count, 3 * blk_dev, block_len)
    local_ids = jnp.arange(blk_dev, dtype=jnp.int32)
    ext_slots = neighbours - neighbours[:, :1] + local_ids[:, None] + blk_dev
    picked = jnp.take(blocks, ext_slots.reshape(-1), axis=1)
    picked = picked.reshape(row_count, blk_dev, neighbours.shape[1], block_len)
    result = jnp.einsum("bkij,xbkj->xbi", near_kernel, picked, preferred_element_type=jnp.float32)
    return result.reshape(row_count, panel_count)


def tree_totals(coeffs):
    narrow_bits = lax.axis_size("narrow").bit_length() - 1
    wide_bits = lax.axis_size("wide").bit_length() - 1
    for bit_pos in range(narrow_bits + wide_bits):
        partner = from_partner(coeffs[bit_pos:], ("wide", "narrow"), bit_pos)
        coeffs = jnp.concatenate([coeffs[:bit_pos], coeffs[bit_pos:] + partner], axis=0)
    return coeffs


def level_gains(panel_count, level_count, rank_len):
    gain_list = [
        0.64 / math.sqrt(rank_len * panel_count * 2 ** (tree_level + 1))
        for tree_level in range(level_count)
    ]
    return jnp.array(gain_list, jnp.float32)


def far_field(field_low, far_basis):
    coeffs = jnp.einsum("xp,lpr->lxr", field_low, far_basis, preferred_element_type=jnp.float32)
    summed = tree_totals(coeffs)
    gains = level_gains(field_low.shape[1], far_basis.shape[0], far_basis.shape[2])
    scaled = (summed * gains[:, None, None]).astype(jnp.bfloat16)
    return jnp.einsum("lxr,lpr->xp", scaled, far_basis, preferred_element_type=jnp.float32)


def apply_operator(field, near_kernel, neighbours, far_basis):
    field_low = field.astype(jnp.bfloat16)
    return near_field(field_low, near_kernel, neighbours) + far_field(field_low, far_basis)


def project_cone(trial_point, mu_sorted):
    normal = trial_point[0]
    slide_a = trial_point[1]
    slide_b = trial_point[2]
    slip = jnp.sqrt(slide_a * slide_a + slide_b * slide_b + SLIP_EPS)
    coeff = mu_sorted[None, :]
    stick = slip <= coeff * normal
    pressed = jnp.where(
        stick, normal, jnp.maximum((normal + coeff * slip) / (1.0 + coeff * coeff), 0.0)
    )
    factor = jnp.where(stick, jnp.ones_like(slip), coeff * pressed / slip)
    return jnp.stack([pressed, factor * slide_a, factor * slide_b])


def body(
    traction,
    near_kernel,
    neighbours,
    far_basis,
    surface_gap,
    friction,
    contact_flags,
    cluster_order,
    approach,
):
    comp_count, load_count, panel_count = traction.shape
    row_count = comp_count * load_count
    local_order = cluster_order % panel_count
    gap_sorted = jnp.take(surface_gap, local_order, axis=1)
    mu_sorted = jnp.take(friction, local_order)
    live_mask = jnp.take(contact_flags, local_order).astype(jnp.float32)
    target = (approach[:, :, None] - gap_sorted[:, None, :]).reshape(row_count, panel_count)
    state_rows = traction.reshape(row_count, panel_count)
    residual = apply_operator(state_rows, near_kernel, neighbours, far_basis) - target
    image_rows = apply_operator(residual, near_kernel, neighbours, far_basis)
    residual_out = residual.reshape(comp_count, load_count, panel_count)
    image_out = image_rows.reshape(comp_count, load_count, panel_count)
    cross_local = jnp.sum(residual_out * image_out, axis=(0, 2))
    square_local = jnp.sum(image_out * image_out, axis=(0, 2))
    cross_sum, square_sum = lax.psum((cross_local, square_local), ("wide", "narrow"))
    entries = comp_count * panel_count * lax.axis_size(("wide", "narrow"))
    step_size = cross_sum / entries / (square_sum / entries + 1e-06)
    trial_point = traction - step_size[None, :, None] * residual_out
    updated = project_cone(trial_point, mu_sorted) * live_mask[None, None, :]
    return (updated, residual_out, step_size)


def solution(mesh):
    return jax.shard_map(
        body,
        mesh=mesh,
        in_specs=(
            P(None, None, ("wide", "narrow")),
            P(("wide", "narrow"), None, None, None),
            P(("wide", "narrow"), None),
            P(None, ("wide", "narrow"), None),
            P(None, ("wide", "narrow")),
            P(("wide", "narrow")),
            P(("wide", "narrow")),
            P(("wide", "narrow")),
            P(),
        ),
        out_specs=(P(None, None, ("wide", "narrow")), P(None, None, ("wide", "narrow")), P()),
        check_vma=False,
    )
```

profile of v0, /device:TPU:14, one launch (start us, length us, event | category | flops | bytes accessed | tf_op | source)
XLA Modules:
  0.0 200.4 jit_solution(18257478556729925627)
XLA Ops:
  2.1 2.4 %collective-permute-start.1 = (bf16[192,1536]{1,0:T(8,128)(2,1)S(1)}, bf16[192,1536]{1,0:T(8,128)(2,1)}, u32[]{:S(2)}, u32[]{:S(2)}) collective-permute-start(bf16[192,1536]{1,0:T(8,128)(2,1)S(1)} %bitcast.62), channel_id=1, source_target_pairs={{1,0},{2,1},{3,2},{4,3},{5,4},{6,5},{7,6},{8,7},{9,8},{10,9},{11,1... | collective-permute-start | bytes 1769480 | tf_op jit(solution)/shard_map/ppermute | solution.py:20
  4.6 4.0 %collective-permute-start = (bf16[192,1536]{1,0:T(8,128)(2,1)S(1)}, bf16[192,1536]{1,0:T(8,128)(2,1)}, u32[]{:S(2)}, u32[]{:S(2)}) collective-permute-start(bf16[192,1536]{1,0:T(8,128)(2,1)S(1)} %bitcast.63), channel_id=1, source_target_pairs={{0,1},{1,2},{2,3},{3,4},{4,5},{5,6},{6,7},{7,8},{8,9},{9,10},{10,1... | collective-permute-start | bytes 1769480 | tf_op jit(solution)/shard_map/ppermute | solution.py:18
  10.4 3.7 %gather_fusion = f32[1536,3]{1,0:T(8,128)} fusion(f32[3,1536]{0,1:T(8,128)S(1)} %copy.40, s32[2048]{0:T(1024)S(1)} %pad_clamp_fusion), kind=kCustom, calls=%fused_computation.2 | custom fusion | bytes 43008 | tf_op jit(solution)/shard_map/jit(_take)/gather | solution.py:109
  14.1 8.4 %gather_fusion.2 = s32[1536]{0:T(1024)S(1)} fusion(s32[1536]{0:T(1024)S(1)} %copy-done.1, s32[2048]{0:T(1024)S(1)} %pad_clamp_fusion), kind=kCustom, calls=%fused_computation.4 | custom fusion | bytes 18432 | tf_op jit(solution)/shard_map/jit(_take)/gather | solution.py:111
  25.8 16.5 %collective-permute-done.2 = f32[5,192,128]{2,1,0:T(8,128)} collective-permute-done((f32[5,192,128]{2,1,0:T(8,128)}, f32[5,192,128]{2,1,0:T(8,128)}, u32[]{:S(2)}, u32[]{:S(2)}) %collective-permute-start.2) | collective-permute-done | bytes 491552 | tf_op jit(solution)/shard_map/ppermute | solution.py:34
  43.7 2.6 %pad_maximum_fusion = bf16[192,4608]{1,0:T(8,128)(2,1)} fusion(bf16[192,1536]{1,0:T(8,128)(2,1)} %collective-permute-done.1, bf16[192,1536]{1,0:T(8,128)(2,1)S(1)} %bitcast.65, bf16[192,1536]{1,0:T(8,128)(2,1)} %collective-permute-done), kind=kLoop, calls=%fused_computation.12 | loop fusion | flops 5308416 | bytes 3538944 | tf_op jit(solution)/shard_map/concatenate | solution.py:16
  46.3 4.0 %copy.37 = bf16[192,4608]{0,1:T(8,128)(2,1)} copy(bf16[192,4608]{1,0:T(8,128)(2,1)} %pad_maximum_fusion) | data formatting | bytes 3538944 | tf_op jit(solution)/shard_map/concatenate | solution.py:16
  50.3 4.0 %copy.38 = bf16[192,9,512]{2,0,1:T(8,128)(2,1)} copy(bf16[192,9,512]{0,2,1:T(8,128)(2,1)} %bitcast.60) | data formatting | bytes 3538944 | tf_op jit(solution)/shard_map/reshape | solution.py:42
  54.4 3.7 %gather_fusion.3 = bf16[12,192,512]{2,1,0:T(8,128)(2,1)} fusion(bf16[192,9,512]{2,0,1:T(8,128)(2,1)} %copy.38, s32[1024]{0:T(1024)S(1)} %pad_clamp_fusion.1), kind=kCustom, calls=%fused_computation.clone | custom fusion | bytes 4718640 | tf_op jit(solution)/shard_map/jit(_take)/gather | solution.py:45
  63.3 5.0 %convolution_bitcast_fusion.3 = f32[3,24,8,512]{3,2,1,0:T(8,128)S(1)} fusion(bf16[192,3,4,512]{3,0,2,1:T(8,128)(2,1)S(1)} %bitcast.59, bf16[3,4,512,512]{3,2,1,0:T(8,128)(2,1)} %param.14), kind=kOutput, calls=%fused_computation.15 | convolution fusion | flops 1207959552 | bytes 9830400 | tf_op jit(solution)/shard_map/bkij,xbkj->xbi/dot_general | solution.py:47
  71.3 4.1 %collective-permute-done.6 = f32[1,192,128]{2,1,0:T(8,128)S(1)} collective-permute-done((f32[1,192,128]{2,1,0:T(8,128)S(1)}, f32[1,192,128]{2,1,0:T(8,128)S(1)}, u32[]{:S(2)}, u32[]{:S(2)}) %collective-permute-start.6) | collective-permute-done | bytes 98336 | tf_op jit(solution)/shard_map/ppermute | solution.py:34
  77.1 2.8 %collective-permute-start.8 = (bf16[192,1536]{1,0:T(8,128)(2,1)}, bf16[192,1536]{1,0:T(8,128)(2,1)}, u32[]{:S(2)}, u32[]{:S(2)}) collective-permute-start(bf16[192,1536]{1,0:T(8,128)(2,1)} %get-tuple-element.15), channel_id=1, source_target_pairs={{1,0},{2,1},{3,2},{4,3},{5,4},{6,5},{7,6},{8,7},{9,8},{10,9},{11,1... | collective-permute-start | bytes 1769480 | tf_op jit(solution)/shard_map/ppermute | solution.py:20
  79.9 3.8 %collective-permute-start.7 = (bf16[192,1536]{1,0:T(8,128)(2,1)}, bf16[192,1536]{1,0:T(8,128)(2,1)}, u32[]{:S(2)}, u32[]{:S(2)}) collective-permute-start(bf16[192,1536]{1,0:T(8,128)(2,1)} %get-tuple-element.15), channel_id=1, source_target_pairs={{0,1},{1,2},{2,3},{3,4},{4,5},{5,6},{6,7},{7,8},{8,9},{9,10},{10,1... | collective-permute-start | bytes 1769480 | tf_op jit(solution)/shard_map/ppermute | solution.py:18
  83.7 2.5 %convolution_bitcast_fusion.5 = f32[5,192,128]{2,1,0:T(8,128)} fusion(bf16[5,1536,128]{2,1,0:T(8,128)(2,1)S(1)} %copy-done, bf16[192,1536]{1,0:T(8,128)(2,1)} %get-tuple-element.15), kind=kOutput, calls=%fused_computation.17 | convolution fusion | flops 377487360 | bytes 3047424 | tf_op jit(solution)/shard_map/xp,lpr->lxr/dot_general | solution.py:69
  86.8 8.4 %gather_fusion.1 = f32[1536]{0:T(1024)S(1)} fusion(f32[1536]{0:T(1024)S(1)} %copy-done.2, s32[2048]{0:T(1024)S(1)} %pad_clamp_fusion), kind=kCustom, calls=%fused_computation.3 | custom fusion | bytes 18432 | tf_op jit(solution)/shard_map/jit(_take)/gather | solution.py:110
  95.7 23.1 %collective-permute-done.9 = f32[5,192,128]{2,1,0:T(8,128)} collective-permute-done((f32[5,192,128]{2,1,0:T(8,128)}, f32[5,192,128]{2,1,0:T(8,128)}, u32[]{:S(2)}, u32[]{:S(2)}) %collective-permute-start.9) | collective-permute-done | bytes 491552 | tf_op jit(solution)/shard_map/ppermute | solution.py:34
  120.8 2.7 %pad_maximum_fusion.1 = bf16[192,4608]{1,0:T(8,128)(2,1)} fusion(bf16[192,1536]{1,0:T(8,128)(2,1)} %collective-permute-done.8, bf16[192,1536]{1,0:T(8,128)(2,1)} %get-tuple-element.15, bf16[192,1536]{1,0:T(8,128)(2,1)} %collective-permute-done.7), kind=kLoop, calls=%fused_computation.13 | loop fusion | flops 5308416 | bytes 3538944 | tf_op jit(solution)/shard_map/concatenate | solution.py:16
  123.6 4.0 %copy.42 = bf16[192,4608]{0,1:T(8,128)(2,1)} copy(bf16[192,4608]{1,0:T(8,128)(2,1)} %pad_maximum_fusion.1) | data formatting | bytes 3538944 | tf_op jit(solution)/shard_map/concatenate | solution.py:16
  127.6 4.0 %copy.43 = bf16[192,9,512]{2,0,1:T(8,128)(2,1)} copy(bf16[192,9,512]{0,2,1:T(8,128)(2,1)} %bitcast.61) | data formatting | bytes 3538944 | tf_op jit(solution)/shard_map/reshape | solution.py:42
  131.6 3.8 %gather_fusion.4 = bf16[12,192,512]{2,1,0:T(8,128)(2,1)} fusion(bf16[192,9,512]{2,0,1:T(8,128)(2,1)} %copy.43, s32[1024]{0:T(1024)} %copy-done.11), kind=kCustom, calls=%fused_computation.1.clone | custom fusion | bytes 4718640 | tf_op jit(solution)/shard_map/jit(_take)/gather | solution.py:45
  140.8 5.0 %convolution_bitcast_fusion.2 = f32[3,24,8,512]{3,2,1,0:T(8,128)S(1)} fusion(bf16[192,3,4,512]{3,0,2,1:T(8,128)(2,1)S(1)} %bitcast.58, bf16[3,4,512,512]{3,2,1,0:T(8,128)(2,1)} %param.14), kind=kOutput, calls=%fused_computation.14 | convolution fusion | flops 1207959552 | bytes 9830400 | tf_op jit(solution)/shard_map/bkij,xbkj->xbi/dot_general | solution.py:47
  146.2 3.4 %collective-permute-start.13 = (f32[1,192,128]{2,1,0:T(8,128)S(1)}, f32[1,192,128]{2,1,0:T(8,128)S(1)}, u32[]{:S(2)}, u32[]{:S(2)}) collective-permute-start(f32[1,192,128]{2,1,0:T(8,128)S(1)} %slice.108), channel_id=1, source_target_pairs={{0,16},{16,0},{1,17},{17,1},{2,18},{18,2},{3,19},{19,3},{4,20},{20... | collective-permute-start | bytes 294920 | tf_op jit(solution)/shard_map/ppermute | solution.py:34
  149.6 3.9 %collective-permute-done.13 = f32[1,192,128]{2,1,0:T(8,128)S(1)} collective-permute-done((f32[1,192,128]{2,1,0:T(8,128)S(1)}, f32[1,192,128]{2,1,0:T(8,128)S(1)}, u32[]{:S(2)}, u32[]{:S(2)}) %collective-permute-start.13) | collective-permute-done | bytes 98336 | tf_op jit(solution)/shard_map/ppermute | solution.py:34
  154.8 42.6 %all-reduce = (f32[64]{0:T(128)S(1)}, f32[64]{0:T(128)S(1)}) all-reduce(f32[64]{0:T(128)S(1)} %reduce_sum.37, f32[64]{0:T(128)S(1)} %reduce_sum.25), channel_id=1, replica_groups=mesh['wide'=8,'narrow'=4] {'wide','narrow'}, use_global_device_ids=true, to_apply=%region_5.7 | all-reduce | flops 128 | bytes 1024 | tf_op jit(solution)/shard_map/psum | solution.py:120
  (111 shorter events, 30.8 us)
Async XLA Ops:
  0.6 8.0 %copy-start = (bf16[5,1536,128]{2,1,0:T(8,128)(2,1)S(1)}, bf16[5,1536,128]{2,1,0:T(8,128)(2,1)}, u32[]{:S(2)}) copy-start(bf16[5,1536,128]{2,1,0:T(8,128)(2,1)} %param.16) | copy-start | bytes 5898244
  2.1 7.9 %copy-start.9 = (f32[3,1536]{1,0:T(4,128)S(1)}, f32[3,1536]{1,0:T(4,128)}, u32[]{:S(2)}) copy-start(f32[3,1536]{1,0:T(4,128)} %param.17) | copy-start | bytes 55300
  2.1 41.5 %collective-permute-start.1 = (bf16[192,1536]{1,0:T(8,128)(2,1)S(1)}, bf16[192,1536]{1,0:T(8,128)(2,1)}, u32[]{:S(2)}, u32[]{:S(2)}) collective-permute-start(bf16[192,1536]{1,0:T(8,128)(2,1)S(1)} %bitcast.62), channel_id=1, source_target_pairs={{1,0},{2,1},{3,2},{4,3},{5,4},{6,5},{7,6},{8,7},{9,8},{10,9},{11,1... | collective-permute-start | bytes 1769480 | tf_op jit(solution)/shard_map/ppermute | solution.py:20
  4.6 39.1 %collective-permute-start = (bf16[192,1536]{1,0:T(8,128)(2,1)S(1)}, bf16[192,1536]{1,0:T(8,128)(2,1)}, u32[]{:S(2)}, u32[]{:S(2)}) collective-permute-start(bf16[192,1536]{1,0:T(8,128)(2,1)S(1)} %bitcast.63), channel_id=1, source_target_pairs={{0,1},{1,2},{2,3},{3,4},{4,5},{5,6},{6,7},{7,8},{8,9},{9,10},{10,1... | collective-permute-start | bytes 1769480 | tf_op jit(solution)/shard_map/ppermute | solution.py:18
  10.1 32.3 %collective-permute-start.2 = (f32[5,192,128]{2,1,0:T(8,128)}, f32[5,192,128]{2,1,0:T(8,128)}, u32[]{:S(2)}, u32[]{:S(2)}) collective-permute-start(f32[5,192,128]{2,1,0:T(8,128)} %convolution_bitcast_fusion.4), channel_id=1, source_target_pairs={{0,1},{1,0},{2,3},{3,2},{4,5},{5,4},{6,7},{7,6},{8,9},{9,8},{10,11... | collective-permute-start | bytes 1474568 | tf_op jit(solution)/shard_map/ppermute | solution.py:34
  14.1 8.4 %copy-start.10 = (s32[3,4]{1,0:T(4,128)S(1)}, s32[3,4]{1,0:T(4,128)}, u32[]{:S(2)}) copy-start(s32[3,4]{1,0:T(4,128)} %param.15) | copy-start | bytes 148
  25.8 28.6 %copy-start.11 = (s32[1024]{0:T(1024)}, s32[1024]{0:T(1024)S(1)}, u32[]{:S(2)}) copy-start(s32[1024]{0:T(1024)S(1)} %pad_clamp_fusion.1) | copy-start | bytes 12292
  25.8 35.0 %copy-start.12 = (pred[12]{0:T(512)(128)(4,1)}, pred[12]{0:T(512)(128)(4,1)S(1)}, u32[]{:S(2)}) copy-start(pred[12]{0:T(512)(128)(4,1)S(1)} %compare_and_fusion.1) | copy-start | bytes 40
  43.6 14.5 %copy-start.6 = (f32[5,192,128]{2,1,0:T(8,128)}, f32[5,192,128]{2,1,0:T(8,128)S(1)}, u32[]{:S(2)}) copy-start(f32[5,192,128]{2,1,0:T(8,128)S(1)} %add.118) | copy-start | bytes 1474564
  43.6 14.4 %collective-permute-start.3 = (f32[4,192,128]{2,1,0:T(8,128)S(1)}, f32[4,192,128]{2,1,0:T(8,128)}, u32[]{:S(2)}, u32[]{:S(2)}) collective-permute-start(f32[4,192,128]{2,1,0:T(8,128)S(1)} %slice.100), channel_id=1, source_target_pairs={{0,2},{2,0},{1,3},{3,1},{4,6},{6,4},{5,7},{7,5},{8,10},{10,8},{9,1... | collective-permute-start | bytes 1179656 | tf_op jit(solution)/shard_map/ppermute | solution.py:34
  59.1 3.6 %collective-permute-start.4 = (f32[3,192,128]{2,1,0:T(8,128)S(1)}, f32[3,192,128]{2,1,0:T(8,128)S(1)}, u32[]{:S(2)}, u32[]{:S(2)}) collective-permute-start(f32[3,192,128]{2,1,0:T(8,128)S(1)} %slice.101), channel_id=1, source_target_pairs={{0,4},{4,0},{1,5},{5,1},{2,6},{6,2},{3,7},{7,3},{8,12},{12,8},{9,1... | collective-permute-start | bytes 884744 | tf_op jit(solution)/shard_map/ppermute | solution.py:34
  62.8 6.9 %collective-permute-start.5 = (f32[2,192,128]{2,1,0:T(8,128)S(1)}, f32[2,192,128]{2,1,0:T(8,128)S(1)}, u32[]{:S(2)}, u32[]{:S(2)}) collective-permute-start(f32[2,192,128]{2,1,0:T(8,128)S(1)} %slice.102), channel_id=1, source_target_pairs={{0,8},{8,0},{1,9},{9,1},{2,10},{10,2},{3,11},{11,3},{4,12},{12,4},... | collective-permute-start | bytes 589832 | tf_op jit(solution)/shard_map/ppermute | solution.py:34
  68.3 7.1 %copy-start.4 = (f32[192,1536]{1,0:T(8,128)S(1)}, f32[192,1536]{1,0:T(8,128)}, u32[]{:S(2)}) copy-start(f32[192,1536]{1,0:T(8,128)} %bitcast_subtract_fusion) | copy-start | bytes 3538948
  69.7 5.7 %collective-permute-start.6 = (f32[1,192,128]{2,1,0:T(8,128)S(1)}, f32[1,192,128]{2,1,0:T(8,128)S(1)}, u32[]{:S(2)}, u32[]{:S(2)}) collective-permute-start(f32[1,192,128]{2,1,0:T(8,128)S(1)} %slice.103), channel_id=1, source_target_pairs={{0,16},{16,0},{1,17},{17,1},{2,18},{18,2},{3,19},{19,3},{4,20},{20... | collective-permute-start | bytes 294920 | tf_op jit(solution)/shard_map/ppermute | solution.py:34
  77.1 120.3 %copy-start.3 = (f32[192,1536]{1,0:T(8,128)}, f32[192,1536]{1,0:T(8,128)S(1)}, u32[]{:S(2)}) copy-start(f32[192,1536]{1,0:T(8,128)S(1)} %get-tuple-element.16) | copy-start | bytes 3538948
  77.1 9.7 %copy-start.2 = (f32[1536]{0:T(1024)S(1)}, f32[1536]{0:T(1024)}, u32[]{:S(2)}) copy-start(f32[1536]{0:T(1024)} %param.18) | copy-start | bytes 18436
  77.1 43.7 %collective-permute-start.8 = (bf16[192,1536]{1,0:T(8,128)(2,1)}, bf16[192,1536]{1,0:T(8,128)(2,1)}, u32[]{:S(2)}, u32[]{:S(2)}) collective-permute-start(bf16[192,1536]{1,0:T(8,128)(2,1)} %get-tuple-element.15), channel_id=1, source_target_pairs={{1,0},{2,1},{3,2},{4,3},{5,4},{6,5},{7,6},{8,7},{9,8},{10,9},{11,1... | collective-permute-start | bytes 1769480 | tf_op jit(solution)/shard_map/ppermute | solution.py:20
  79.9 41.0 %collective-permute-start.7 = (bf16[192,1536]{1,0:T(8,128)(2,1)}, bf16[192,1536]{1,0:T(8,128)(2,1)}, u32[]{:S(2)}, u32[]{:S(2)}) collective-permute-start(bf16[192,1536]{1,0:T(8,128)(2,1)} %get-tuple-element.15), channel_id=1, source_target_pairs={{0,1},{1,2},{2,3},{3,4},{4,5},{5,6},{6,7},{7,8},{8,9},{9,10},{10,1... | collective-permute-start | bytes 1769480 | tf_op jit(solution)/shard_map/ppermute | solution.py:18
  86.2 32.6 %collective-permute-start.9 = (f32[5,192,128]{2,1,0:T(8,128)}, f32[5,192,128]{2,1,0:T(8,128)}, u32[]{:S(2)}, u32[]{:S(2)}) collective-permute-start(f32[5,192,128]{2,1,0:T(8,128)} %convolution_bitcast_fusion.5), channel_id=1, source_target_pairs={{0,1},{1,0},{2,3},{3,2},{4,5},{5,4},{6,7},{7,6},{8,9},{9,8},{10,11... | collective-permute-start | bytes 1474568 | tf_op jit(solution)/shard_map/ppermute | solution.py:34
  120.8 14.6 %collective-permute-start.10 = (f32[4,192,128]{2,1,0:T(8,128)S(1)}, f32[4,192,128]{2,1,0:T(8,128)}, u32[]{:S(2)}, u32[]{:S(2)}) collective-permute-start(f32[4,192,128]{2,1,0:T(8,128)S(1)} %slice.105), channel_id=1, source_target_pairs={{0,2},{2,0},{1,3},{3,1},{4,6},{6,4},{5,7},{7,5},{8,10},{10,8},{9,1... | collective-permute-start | bytes 1179656 | tf_op jit(solution)/shard_map/ppermute | solution.py:34
  136.6 2.1 %collective-permute-start.11 = (f32[3,192,128]{2,1,0:T(8,128)S(1)}, f32[3,192,128]{2,1,0:T(8,128)S(1)}, u32[]{:S(2)}, u32[]{:S(2)}) collective-permute-start(f32[3,192,128]{2,1,0:T(8,128)S(1)} %slice.106), channel_id=1, source_target_pairs={{0,4},{4,0},{1,5},{5,1},{2,6},{6,2},{3,7},{7,3},{8,12},{12,8},{9,1... | collective-permute-start | bytes 884744 | tf_op jit(solution)/shard_map/ppermute | solution.py:34
  138.8 7.4 %collective-permute-start.12 = (f32[2,192,128]{2,1,0:T(8,128)S(1)}, f32[2,192,128]{2,1,0:T(8,128)S(1)}, u32[]{:S(2)}, u32[]{:S(2)}) collective-permute-start(f32[2,192,128]{2,1,0:T(8,128)S(1)} %slice.107), channel_id=1, source_target_pairs={{0,8},{8,0},{1,9},{9,1},{2,10},{10,2},{3,11},{11,3},{4,12},{12,4},... | collective-permute-start | bytes 589832 | tf_op jit(solution)/shard_map/ppermute | solution.py:34
  145.8 7.7 %copy-start.16 = (f32[5]{0:T(128)S(1)}, f32[5]{0:T(128)}, u32[]{:S(2)}) copy-start(f32[5]{0:T(128)} %constant.79.clone) | copy-start | bytes 64
  146.2 7.4 %collective-permute-start.13 = (f32[1,192,128]{2,1,0:T(8,128)S(1)}, f32[1,192,128]{2,1,0:T(8,128)S(1)}, u32[]{:S(2)}, u32[]{:S(2)}) collective-permute-start(f32[1,192,128]{2,1,0:T(8,128)S(1)} %slice.108), channel_id=1, source_target_pairs={{0,16},{16,0},{1,17},{17,1},{2,18},{18,2},{3,19},{19,3},{4,20},{20... | collective-permute-start | bytes 294920 | tf_op jit(solution)/shard_map/ppermute | solution.py:34
  (10 other events, 28.3 us)
where the time goes:
time: 201 us; the launch traced here: 200 us
  waiting for transfers between devices  49.1 us (24%)
  local copies, waits for them, and re-layouts  46.2 us (23%)
  blocking collectives  42.6 us (21%)
  starting transfers between devices  23 us (11%)
  other arithmetic  21.9 us (11%)
  matrix products  16.5 us (8%)
    ppermute x10, waiting for transfers between devices, from_partner(): return lax.ppermute(block, axis, route)  49.1 us
    psum x1, blocking collectives, body(): lax.psum((cross_local, square_local), ('wide', 'narrow'))  42.6 us
    ppermute x10, starting transfers between devices, from_partner(): return lax.ppermute(block, axis, route)  9.93 us
    dot_general x2, matrix products, near_field(): jnp.einsum('bkij,xbkj->xbi', near_kernel, picked, preferred_element_type=...  9.91 us
    gather x1, local copies, waits for them, and re-layouts, body(): live_mask = jnp.take(contact_flags, local_order).astype(jnp.float32)  8.38 us
    gather x1, local copies, waits for them, and re-layouts, body(): mu_sorted = jnp.take(friction, local_order)  8.38 us
    reshape x2, local copies, waits for them, and re-layouts, near_field(): blocks = padded.reshape(row_count, 3 * blk_dev, block_len)  8.08 us
    concatenate x2, local copies, waits for them, and re-layouts, extended(): jnp.concatenate([lax.ppermute(tail, axis, [(i, (i + 1) % count) for i in...  7.99 us
  transfers between devices with their start and end apart: 14, of which 6 were waited for; matrix products, arithmetic and copies ran while one was open for 37% of the time, Pallas kernels for 0%

commit v1 on v0

--- a/solution.py
+++ b/solution.py
@@ -117,7 +117,7 @@
     image_out = image_rows.reshape(comp_count, load_count, panel_count)
     cross_local = jnp.sum(residual_out * image_out, axis=(0, 2))
     square_local = jnp.sum(image_out * image_out, axis=(0, 2))
-    cross_sum, square_sum = lax.psum((cross_local, square_local), ("wide", "narrow"))
+    cross_sum, square_sum = lax.psum(lax.psum((cross_local, square_local), "narrow"), "wide")
     entries = comp_count * panel_count * lax.axis_size(("wide", "narrow"))
     step_size = cross_sum / entries / (square_sum / entries + 1e-06)
     trial_point = traction - step_size[None, :, None] * residual_out

time: 201 us -> 187 us (0.930)
  the two profiles are of different devices: /device:TPU:14 before, /device:TPU:0 now
where the time goes in v1:
time: 187 us; the launch traced here: 185 us
  local copies, waits for them, and re-layouts  46.2 us (25%)
  waiting for transfers between devices  44.4 us (24%)
  starting transfers between devices  30.7 us (16%)
  blocking collectives  24.6 us (13%)
  other arithmetic  21.9 us (12%)
  matrix products  16.5 us (9%)
    ppermute x10, waiting for transfers between devices, from_partner(): return lax.ppermute(block, axis, route)  44.4 us
    ppermute x10, starting transfers between devices, from_partner(): return lax.ppermute(block, axis, route)  16.2 us
    psum x1, blocking collectives, body(): lax.psum(lax.psum((cross_local, square_local), 'narrow'), 'wide')  14.7 us
    ppermute x2, starting transfers between devices, extended(): lax.ppermute(tail, axis, [(i, (i + 1) % count) for i in range(ends)])  11.7 us
    psum x1, blocking collectives, body(): lax.psum((cross_local, square_local), 'narrow')  9.94 us
    dot_general x2, matrix products, near_field(): jnp.einsum('bkij,xbkj->xbi', near_kernel, picked, preferred_element_type=...  9.92 us
    gather x1, local copies, waits for them, and re-layouts, body(): live_mask = jnp.take(contact_flags, local_order).astype(jnp.float32)  8.38 us
    gather x1, local copies, waits for them, and re-layouts, body(): mu_sorted = jnp.take(friction, local_order)  8.38 us
  transfers between devices with their start and end apart: 14, of which 6 were waited for; matrix products, arithmetic and copies ran while one was open for 40% of the time, Pallas kernels for 0%

profile of v1, /device:TPU:0, one launch (start us, length us, event | category | flops | bytes accessed | tf_op | source)
XLA Modules:
  0.0 185.4 jit_solution(11235815945307147678)
XLA Ops:
  3.4 6.3 %collective-permute-start = (bf16[192,1536]{1,0:T(8,128)(2,1)S(1)}, bf16[192,1536]{1,0:T(8,128)(2,1)}, u32[]{:S(2)}, u32[]{:S(2)}) collective-permute-start(bf16[192,1536]{1,0:T(8,128)(2,1)S(1)} %bitcast.63), channel_id=1, source_target_pairs={{0,1},{1,2},{2,3},{3,4},{4,5},{5,6},{6,7},{7,8},{8,9},{9,10},{10,1... | collective-permute-start | bytes 1769480 | tf_op jit(solution)/shard_map/ppermute | solution.py:18
  13.7 3.7 %gather_fusion = f32[1536,3]{1,0:T(8,128)} fusion(f32[3,1536]{0,1:T(8,128)S(1)} %copy.40, s32[2048]{0:T(1024)S(1)} %pad_clamp_fusion), kind=kCustom, calls=%fused_computation.2 | custom fusion | bytes 43008 | tf_op jit(solution)/shard_map/jit(_take)/gather | solution.py:109
  17.4 8.4 %gather_fusion.2 = s32[1536]{0:T(1024)S(1)} fusion(s32[1536]{0:T(1024)S(1)} %copy-done.1, s32[2048]{0:T(1024)S(1)} %pad_clamp_fusion), kind=kCustom, calls=%fused_computation.4 | custom fusion | bytes 18432 | tf_op jit(solution)/shard_map/jit(_take)/gather | solution.py:111
  29.0 14.6 %collective-permute-done.2 = f32[5,192,128]{2,1,0:T(8,128)} collective-permute-done((f32[5,192,128]{2,1,0:T(8,128)}, f32[5,192,128]{2,1,0:T(8,128)}, u32[]{:S(2)}, u32[]{:S(2)}) %collective-permute-start.2) | collective-permute-done | bytes 491552 | tf_op jit(solution)/shard_map/ppermute | solution.py:34
  45.7 2.6 %pad_maximum_fusion = bf16[192,4608]{1,0:T(8,128)(2,1)} fusion(bf16[192,1536]{1,0:T(8,128)(2,1)} %collective-permute-done.1, bf16[192,1536]{1,0:T(8,128)(2,1)S(1)} %bitcast.65, bf16[192,1536]{1,0:T(8,128)(2,1)} %collective-permute-done), kind=kLoop, calls=%fused_computation.12 | loop fusion | flops 5308416 | bytes 3538944 | tf_op jit(solution)/shard_map/concatenate | solution.py:16
  48.3 4.0 %copy.37 = bf16[192,4608]{0,1:T(8,128)(2,1)} copy(bf16[192,4608]{1,0:T(8,128)(2,1)} %pad_maximum_fusion) | data formatting | bytes 3538944 | tf_op jit(solution)/shard_map/concatenate | solution.py:16
  52.2 4.0 %copy.38 = bf16[192,9,512]{2,0,1:T(8,128)(2,1)} copy(bf16[192,9,512]{0,2,1:T(8,128)(2,1)} %bitcast.60) | data formatting | bytes 3538944 | tf_op jit(solution)/shard_map/reshape | solution.py:42
  56.3 3.7 %gather_fusion.3 = bf16[12,192,512]{2,1,0:T(8,128)(2,1)} fusion(bf16[192,9,512]{2,0,1:T(8,128)(2,1)} %copy.38, s32[1024]{0:T(1024)S(1)} %pad_clamp_fusion.1), kind=kCustom, calls=%fused_computation.clone | custom fusion | bytes 4718640 | tf_op jit(solution)/shard_map/jit(_take)/gather | solution.py:45
  65.9 5.0 %convolution_bitcast_fusion.3 = f32[3,24,8,512]{3,2,1,0:T(8,128)S(1)} fusion(bf16[192,3,4,512]{3,0,2,1:T(8,128)(2,1)S(1)} %bitcast.59, bf16[3,4,512,512]{3,2,1,0:T(8,128)(2,1)} %param.14), kind=kOutput, calls=%fused_computation.15 | convolution fusion | flops 1207959552 | bytes 9830400 | tf_op jit(solution)/shard_map/bkij,xbkj->xbi/dot_general | solution.py:47
  71.5 2.8 %collective-permute-start.6 = (f32[1,192,128]{2,1,0:T(8,128)S(1)}, f32[1,192,128]{2,1,0:T(8,128)S(1)}, u32[]{:S(2)}, u32[]{:S(2)}) collective-permute-start(f32[1,192,128]{2,1,0:T(8,128)S(1)} %slice.103), channel_id=1, source_target_pairs={{0,16},{16,0},{1,17},{17,1},{2,18},{18,2},{3,19},{19,3},{4,20},{20... | collective-permute-start | bytes 294920 | tf_op jit(solution)/shard_map/ppermute | solution.py:34
  74.3 4.8 %collective-permute-done.6 = f32[1,192,128]{2,1,0:T(8,128)S(1)} collective-permute-done((f32[1,192,128]{2,1,0:T(8,128)S(1)}, f32[1,192,128]{2,1,0:T(8,128)S(1)}, u32[]{:S(2)}, u32[]{:S(2)}) %collective-permute-start.6) | collective-permute-done | bytes 98336 | tf_op jit(solution)/shard_map/ppermute | solution.py:34
  82.3 5.4 %collective-permute-start.7 = (bf16[192,1536]{1,0:T(8,128)(2,1)}, bf16[192,1536]{1,0:T(8,128)(2,1)}, u32[]{:S(2)}, u32[]{:S(2)}) collective-permute-start(bf16[192,1536]{1,0:T(8,128)(2,1)} %get-tuple-element.17), channel_id=1, source_target_pairs={{0,1},{1,2},{2,3},{3,4},{4,5},{5,6},{6,7},{7,8},{8,9},{9,10},{10,1... | collective-permute-start | bytes 1769480 | tf_op jit(solution)/shard_map/ppermute | solution.py:18
  87.7 2.5 %convolution_bitcast_fusion.5 = f32[5,192,128]{2,1,0:T(8,128)} fusion(bf16[5,1536,128]{2,1,0:T(8,128)(2,1)S(1)} %copy-done, bf16[192,1536]{1,0:T(8,128)(2,1)} %get-tuple-element.17), kind=kOutput, calls=%fused_computation.17 | convolution fusion | flops 377487360 | bytes 3047424 | tf_op jit(solution)/shard_map/xp,lpr->lxr/dot_general | solution.py:69
  91.6 8.4 %gather_fusion.1 = f32[1536]{0:T(1024)S(1)} fusion(f32[1536]{0:T(1024)S(1)} %copy-done.2, s32[2048]{0:T(1024)S(1)} %pad_clamp_fusion), kind=kCustom, calls=%fused_computation.3 | custom fusion | bytes 18432 | tf_op jit(solution)/shard_map/jit(_take)/gather | solution.py:110
  100.6 19.1 %collective-permute-done.9 = f32[5,192,128]{2,1,0:T(8,128)} collective-permute-done((f32[5,192,128]{2,1,0:T(8,128)}, f32[5,192,128]{2,1,0:T(8,128)}, u32[]{:S(2)}, u32[]{:S(2)}) %collective-permute-start.9) | collective-permute-done | bytes 491552 | tf_op jit(solution)/shard_map/ppermute | solution.py:34
  121.7 2.8 %pad_maximum_fusion.1 = bf16[192,4608]{1,0:T(8,128)(2,1)} fusion(bf16[192,1536]{1,0:T(8,128)(2,1)} %collective-permute-done.8, bf16[192,1536]{1,0:T(8,128)(2,1)} %get-tuple-element.17, bf16[192,1536]{1,0:T(8,128)(2,1)} %collective-permute-done.7), kind=kLoop, calls=%fused_computation.13 | loop fusion | flops 5308416 | bytes 3538944 | tf_op jit(solution)/shard_map/concatenate | solution.py:16
  124.5 4.0 %copy.42 = bf16[192,4608]{0,1:T(8,128)(2,1)} copy(bf16[192,4608]{1,0:T(8,128)(2,1)} %pad_maximum_fusion.1) | data formatting | bytes 3538944 | tf_op jit(solution)/shard_map/concatenate | solution.py:16
  128.5 4.0 %copy.43 = bf16[192,9,512]{2,0,1:T(8,128)(2,1)} copy(bf16[192,9,512]{0,2,1:T(8,128)(2,1)} %bitcast.61) | data formatting | bytes 3538944 | tf_op jit(solution)/shard_map/reshape | solution.py:42
  132.5 3.8 %gather_fusion.4 = bf16[12,192,512]{2,1,0:T(8,128)(2,1)} fusion(bf16[192,9,512]{2,0,1:T(8,128)(2,1)} %copy.43, s32[1024]{0:T(1024)} %copy-done.11), kind=kCustom, calls=%fused_computation.1.clone | custom fusion | bytes 4718640 | tf_op jit(solution)/shard_map/jit(_take)/gather | solution.py:45
  142.5 5.0 %convolution_bitcast_fusion.2 = f32[3,24,8,512]{3,2,1,0:T(8,128)S(1)} fusion(bf16[192,3,4,512]{3,0,2,1:T(8,128)(2,1)S(1)} %bitcast.58, bf16[3,4,512,512]{3,2,1,0:T(8,128)(2,1)} %param.14), kind=kOutput, calls=%fused_computation.14 | convolution fusion | flops 1207959552 | bytes 9830400 | tf_op jit(solution)/shard_map/bkij,xbkj->xbi/dot_general | solution.py:47
  148.1 3.4 %collective-permute-start.13 = (f32[1,192,128]{2,1,0:T(8,128)S(1)}, f32[1,192,128]{2,1,0:T(8,128)S(1)}, u32[]{:S(2)}, u32[]{:S(2)}) collective-permute-start(f32[1,192,128]{2,1,0:T(8,128)S(1)} %slice.108), channel_id=1, source_target_pairs={{0,16},{16,0},{1,17},{17,1},{2,18},{18,2},{3,19},{19,3},{4,20},{20... | collective-permute-start | bytes 294920 | tf_op jit(solution)/shard_map/ppermute | solution.py:34
  151.5 5.0 %collective-permute-done.13 = f32[1,192,128]{2,1,0:T(8,128)S(1)} collective-permute-done((f32[1,192,128]{2,1,0:T(8,128)S(1)}, f32[1,192,128]{2,1,0:T(8,128)S(1)}, u32[]{:S(2)}, u32[]{:S(2)}) %collective-permute-start.13) | collective-permute-done | bytes 98336 | tf_op jit(solution)/shard_map/ppermute | solution.py:34
  157.7 9.9 %all-reduce.1 = (f32[64]{0:T(128)S(1)}, f32[64]{0:T(128)S(1)}) all-reduce(f32[64]{0:T(128)S(1)} %reduce_sum.37, f32[64]{0:T(128)S(1)} %reduce_sum.25), channel_id=1, replica_groups=mesh['wide'=8,'narrow'=4] {'narrow'}, use_global_device_ids=true, to_apply=%region_6.8 | all-reduce | flops 128 | bytes 1024 | tf_op jit(solution)/shard_map/psum | solution.py:120
  167.7 14.7 %all-reduce = (f32[64]{0:T(128)S(1)}, f32[64]{0:T(128)S(1)}) all-reduce(f32[64]{0:T(128)S(1)} %get-tuple-element.8, f32[64]{0:T(128)S(1)} %get-tuple-element.9), channel_id=1, replica_groups=mesh['wide'=8,'narrow'=4] {'wide'}, use_global_device_ids=true, to_apply=%region_7.9 | all-reduce | flops 128 | bytes 1024 | tf_op jit(solution)/shard_map/psum | solution.py:120
  (112 shorter events, 36.4 us)
Async XLA Ops:
  0.6 9.2 %copy-start = (bf16[5,1536,128]{2,1,0:T(8,128)(2,1)S(1)}, bf16[5,1536,128]{2,1,0:T(8,128)(2,1)}, u32[]{:S(2)}) copy-start(bf16[5,1536,128]{2,1,0:T(8,128)(2,1)} %param.16) | copy-start | bytes 5898244
  2.1 11.2 %copy-start.9 = (f32[3,1536]{1,0:T(4,128)S(1)}, f32[3,1536]{1,0:T(4,128)}, u32[]{:S(2)}) copy-start(f32[3,1536]{1,0:T(4,128)} %param.17) | copy-start | bytes 55300
  2.1 43.5 %collective-permute-start.1 = (bf16[192,1536]{1,0:T(8,128)(2,1)S(1)}, bf16[192,1536]{1,0:T(8,128)(2,1)}, u32[]{:S(2)}, u32[]{:S(2)}) collective-permute-start(bf16[192,1536]{1,0:T(8,128)(2,1)S(1)} %bitcast.62), channel_id=1, source_target_pairs={{1,0},{2,1},{3,2},{4,3},{5,4},{6,5},{7,6},{8,7},{9,8},{10,9},{11,1... | collective-permute-start | bytes 1769480 | tf_op jit(solution)/shard_map/ppermute | solution.py:20
  3.4 42.2 %collective-permute-start = (bf16[192,1536]{1,0:T(8,128)(2,1)S(1)}, bf16[192,1536]{1,0:T(8,128)(2,1)}, u32[]{:S(2)}, u32[]{:S(2)}) collective-permute-start(bf16[192,1536]{1,0:T(8,128)(2,1)S(1)} %bitcast.63), channel_id=1, source_target_pairs={{0,1},{1,2},{2,3},{3,4},{4,5},{5,6},{6,7},{7,8},{8,9},{9,10},{10,1... | collective-permute-start | bytes 1769480 | tf_op jit(solution)/shard_map/ppermute | solution.py:18
  11.2 32.4 %collective-permute-start.2 = (f32[5,192,128]{2,1,0:T(8,128)}, f32[5,192,128]{2,1,0:T(8,128)}, u32[]{:S(2)}, u32[]{:S(2)}) collective-permute-start(f32[5,192,128]{2,1,0:T(8,128)} %convolution_bitcast_fusion.4), channel_id=1, source_target_pairs={{0,1},{1,0},{2,3},{3,2},{4,5},{5,4},{6,7},{7,6},{8,9},{9,8},{10,11... | collective-permute-start | bytes 1474568 | tf_op jit(solution)/shard_map/ppermute | solution.py:34
  17.4 8.4 %copy-start.10 = (s32[3,4]{1,0:T(4,128)S(1)}, s32[3,4]{1,0:T(4,128)}, u32[]{:S(2)}) copy-start(s32[3,4]{1,0:T(4,128)} %param.15) | copy-start | bytes 148
  29.0 27.3 %copy-start.11 = (s32[1024]{0:T(1024)}, s32[1024]{0:T(1024)S(1)}, u32[]{:S(2)}) copy-start(s32[1024]{0:T(1024)S(1)} %pad_clamp_fusion.1) | copy-start | bytes 12292
  29.0 32.4 %copy-start.12 = (pred[12]{0:T(512)(128)(4,1)}, pred[12]{0:T(512)(128)(4,1)S(1)}, u32[]{:S(2)}) copy-start(pred[12]{0:T(512)(128)(4,1)S(1)} %compare_and_fusion.1) | copy-start | bytes 40
  44.8 15.2 %copy-start.6 = (f32[5,192,128]{2,1,0:T(8,128)}, f32[5,192,128]{2,1,0:T(8,128)S(1)}, u32[]{:S(2)}) copy-start(f32[5,192,128]{2,1,0:T(8,128)S(1)} %add.122) | copy-start | bytes 1474564
  44.9 15.1 %collective-permute-start.3 = (f32[4,192,128]{2,1,0:T(8,128)S(1)}, f32[4,192,128]{2,1,0:T(8,128)}, u32[]{:S(2)}, u32[]{:S(2)}) collective-permute-start(f32[4,192,128]{2,1,0:T(8,128)S(1)} %slice.100), channel_id=1, source_target_pairs={{0,2},{2,0},{1,3},{3,1},{4,6},{6,4},{5,7},{7,5},{8,10},{10,8},{9,1... | collective-permute-start | bytes 1179656 | tf_op jit(solution)/shard_map/ppermute | solution.py:34
  61.1 2.3 %collective-permute-start.4 = (f32[3,192,128]{2,1,0:T(8,128)S(1)}, f32[3,192,128]{2,1,0:T(8,128)S(1)}, u32[]{:S(2)}, u32[]{:S(2)}) collective-permute-start(f32[3,192,128]{2,1,0:T(8,128)S(1)} %slice.101), channel_id=1, source_target_pairs={{0,4},{4,0},{1,5},{5,1},{2,6},{6,2},{3,7},{7,3},{8,12},{12,8},{9,1... | collective-permute-start | bytes 884744 | tf_op jit(solution)/shard_map/ppermute | solution.py:34
  63.4 8.0 %collective-permute-start.5 = (f32[2,192,128]{2,1,0:T(8,128)S(1)}, f32[2,192,128]{2,1,0:T(8,128)S(1)}, u32[]{:S(2)}, u32[]{:S(2)}) collective-permute-start(f32[2,192,128]{2,1,0:T(8,128)S(1)} %slice.102), channel_id=1, source_target_pairs={{0,8},{8,0},{1,9},{9,1},{2,10},{10,2},{3,11},{11,3},{4,12},{12,4},... | collective-permute-start | bytes 589832 | tf_op jit(solution)/shard_map/ppermute | solution.py:34
  70.9 8.3 %copy-start.4 = (f32[192,1536]{1,0:T(8,128)S(1)}, f32[192,1536]{1,0:T(8,128)}, u32[]{:S(2)}) copy-start(f32[192,1536]{1,0:T(8,128)} %bitcast_subtract_fusion) | copy-start | bytes 3538948
  71.5 7.7 %collective-permute-start.6 = (f32[1,192,128]{2,1,0:T(8,128)S(1)}, f32[1,192,128]{2,1,0:T(8,128)S(1)}, u32[]{:S(2)}, u32[]{:S(2)}) collective-permute-start(f32[1,192,128]{2,1,0:T(8,128)S(1)} %slice.103), channel_id=1, source_target_pairs={{0,16},{16,0},{1,17},{17,1},{2,18},{18,2},{3,19},{19,3},{4,20},{20... | collective-permute-start | bytes 294920 | tf_op jit(solution)/shard_map/ppermute | solution.py:34
  80.9 101.5 %copy-start.3 = (f32[192,1536]{1,0:T(8,128)}, f32[192,1536]{1,0:T(8,128)S(1)}, u32[]{:S(2)}) copy-start(f32[192,1536]{1,0:T(8,128)S(1)} %get-tuple-element.18) | copy-start | bytes 3538948
  80.9 10.7 %copy-start.2 = (f32[1536]{0:T(1024)S(1)}, f32[1536]{0:T(1024)}, u32[]{:S(2)}) copy-start(f32[1536]{0:T(1024)} %param.18) | copy-start | bytes 18436
  80.9 40.8 %collective-permute-start.8 = (bf16[192,1536]{1,0:T(8,128)(2,1)}, bf16[192,1536]{1,0:T(8,128)(2,1)}, u32[]{:S(2)}, u32[]{:S(2)}) collective-permute-start(bf16[192,1536]{1,0:T(8,128)(2,1)} %get-tuple-element.17), channel_id=1, source_target_pairs={{1,0},{2,1},{3,2},{4,3},{5,4},{6,5},{7,6},{8,7},{9,8},{10,9},{11,1... | collective-permute-start | bytes 1769480 | tf_op jit(solution)/shard_map/ppermute | solution.py:20
  82.3 39.4 %collective-permute-start.7 = (bf16[192,1536]{1,0:T(8,128)(2,1)}, bf16[192,1536]{1,0:T(8,128)(2,1)}, u32[]{:S(2)}, u32[]{:S(2)}) collective-permute-start(bf16[192,1536]{1,0:T(8,128)(2,1)} %get-tuple-element.17), channel_id=1, source_target_pairs={{0,1},{1,2},{2,3},{3,4},{4,5},{5,6},{6,7},{7,8},{8,9},{9,10},{10,1... | collective-permute-start | bytes 1769480 | tf_op jit(solution)/shard_map/ppermute | solution.py:18
  90.2 29.5 %collective-permute-start.9 = (f32[5,192,128]{2,1,0:T(8,128)}, f32[5,192,128]{2,1,0:T(8,128)}, u32[]{:S(2)}, u32[]{:S(2)}) collective-permute-start(f32[5,192,128]{2,1,0:T(8,128)} %convolution_bitcast_fusion.5), channel_id=1, source_target_pairs={{0,1},{1,0},{2,3},{3,2},{4,5},{5,4},{6,7},{7,6},{8,9},{9,8},{10,11... | collective-permute-start | bytes 1474568 | tf_op jit(solution)/shard_map/ppermute | solution.py:34
  121.7 14.6 %collective-permute-start.10 = (f32[4,192,128]{2,1,0:T(8,128)S(1)}, f32[4,192,128]{2,1,0:T(8,128)}, u32[]{:S(2)}, u32[]{:S(2)}) collective-permute-start(f32[4,192,128]{2,1,0:T(8,128)S(1)} %slice.105), channel_id=1, source_target_pairs={{0,2},{2,0},{1,3},{3,1},{4,6},{6,4},{5,7},{7,5},{8,10},{10,8},{9,1... | collective-permute-start | bytes 1179656 | tf_op jit(solution)/shard_map/ppermute | solution.py:34
  137.5 3.3 %collective-permute-start.11 = (f32[3,192,128]{2,1,0:T(8,128)S(1)}, f32[3,192,128]{2,1,0:T(8,128)S(1)}, u32[]{:S(2)}, u32[]{:S(2)}) collective-permute-start(f32[3,192,128]{2,1,0:T(8,128)S(1)} %slice.106), channel_id=1, source_target_pairs={{0,4},{4,0},{1,5},{5,1},{2,6},{6,2},{3,7},{7,3},{8,12},{12,8},{9,1... | collective-permute-start | bytes 884744 | tf_op jit(solution)/shard_map/ppermute | solution.py:34
  140.9 7.1 %collective-permute-start.12 = (f32[2,192,128]{2,1,0:T(8,128)S(1)}, f32[2,192,128]{2,1,0:T(8,128)S(1)}, u32[]{:S(2)}, u32[]{:S(2)}) collective-permute-start(f32[2,192,128]{2,1,0:T(8,128)S(1)} %slice.107), channel_id=1, source_target_pairs={{0,8},{8,0},{1,9},{9,1},{2,10},{10,2},{3,11},{11,3},{4,12},{12,4},... | collective-permute-start | bytes 589832 | tf_op jit(solution)/shard_map/ppermute | solution.py:34
  147.4 9.1 %copy-start.16 = (f32[5]{0:T(128)S(1)}, f32[5]{0:T(128)}, u32[]{:S(2)}) copy-start(f32[5]{0:T(128)} %constant.79.clone) | copy-start | bytes 64
  148.1 8.4 %collective-permute-start.13 = (f32[1,192,128]{2,1,0:T(8,128)S(1)}, f32[1,192,128]{2,1,0:T(8,128)S(1)}, u32[]{:S(2)}, u32[]{:S(2)}) collective-permute-start(f32[1,192,128]{2,1,0:T(8,128)S(1)} %slice.108), channel_id=1, source_target_pairs={{0,16},{16,0},{1,17},{17,1},{2,18},{18,2},{3,19},{19,3},{4,20},{20... | collective-permute-start | bytes 294920 | tf_op jit(solution)/shard_map/ppermute | solution.py:34
  (10 other events, 35.6 us)
